TPU v7x, 512 devices: a whole 4x8x8 slice. The times are simulated.
512 devices in a mesh: tok: 16 (over z, y_hi), hid: 32 (over y_lo, x, core).
Axes of the slice: x: 4, y: 8 (y_hi: 2, y_lo: 4; y = y_hi * 4 + y_lo), z: 8, core: 2. Of those that a mesh axis runs over, the one named last changes fastest.
Arguments:
- resid_in: bfloat16 [512, 8192], P('hid', 'tok'), may hold values from -64 to 64
- norm_gain: float32 [8192], P('tok'), may hold values from 0.1 to 1.9
- gate_weight: bfloat16 [8192, 28672], P('tok', 'hid'), may hold values from -0.0625 to 0.0625
- up_weight: bfloat16 [8192, 28672], P('tok', 'hid'), may hold values from -0.0625 to 0.0625
- down_weight: bfloat16 [28672, 8192], P('hid', 'tok'), may hold values from -0.0625 to 0.0625
- labels: int32 [512], replicated, may hold values from 0 to 63
Outputs:
- gram: float32 [8192, 8192], P(('tok', 'hid'))
- cross: float32 [8192, 64], P(('tok', 'hid'))
All inputs are finite; a program needn't handle non-finite values.
Results may differ from a plain program's by a relative error of at most 0.014.
Values may be sent and summed in bfloat16 or wider, within the bound.
A program may use at most 64 MiB of HBM per device.

v0:
```python
import jax
import jax.numpy as jnp
from jax import lax
from jax.sharding import PartitionSpec as P

D = 8192
CLASSES = 64


def on_device(resid_in, norm_gain, gate_weight, up_weight, down_weight, labels):
    gathered = lax.all_gather(resid_in, "hid", axis=0, tiled=True)
    xf = gathered.astype(jnp.float32)
    local_sq = jnp.sum(xf * xf, axis=1)
    total_sq = lax.psum(local_sq, "tok")
    scale_rows = lax.rsqrt(total_sq / float(D) + 1e-05)
    normed = (xf * scale_rows[:, None] * norm_gain[None, :]).astype(jnp.bfloat16)
    both_weights = jnp.concatenate([gate_weight, up_weight], axis=1)
    shard_ff = gate_weight.shape[1]
    paired = lax.psum_scatter(
        jnp.dot(normed, both_weights, preferred_element_type=jnp.float32).astype(jnp.bfloat16),
        "tok",
        scatter_dimension=0,
        tiled=True,
    ).astype(jnp.float32)
    hidden = (jax.nn.silu(paired[:, :shard_ff]) * paired[:, shard_ff:]).astype(jnp.bfloat16)
    partial_out = jnp.dot(
        lax.all_gather(hidden, "tok", axis=0, tiled=True),
        down_weight,
        preferred_element_type=jnp.float32,
    )
    ntok = xf.shape[0]
    panel = xf.shape[1] // lax.axis_size("hid")
    offset = lax.axis_index("hid") * panel
    summed = lax.psum_scatter(
        partial_out.astype(jnp.bfloat16), "hid", scatter_dimension=1, tiled=True
    ).astype(jnp.float32)
    x_cols = lax.dynamic_slice_in_dim(xf, offset, panel, 1)
    resid_cols = (x_cols + summed).astype(jnp.bfloat16)
    prod = lax.dot_general(
        resid_cols,
        lax.all_gather(resid_cols, ("tok", "hid"), axis=1, tiled=True),
        (((0,), (0,)), ((), ())),
        preferred_element_type=jnp.float32,
    )
    gram = prod / float(ntok)
    onehot = (labels[:, None] == jnp.arange(CLASSES, dtype=jnp.int32)[None, :]).astype(jnp.bfloat16)
    counts = jnp.sum(onehot.astype(jnp.float32), axis=0)
    class_sums = lax.dot_general(
        resid_cols, onehot, (((0,), (0,)), ((), ())), preferred_element_type=jnp.float32
    )
    cross = class_sums / jnp.maximum(counts, 1.0)[None, :]
    return (gram, cross)


def solution(mesh):
    return jax.shard_map(
        on_device,
        mesh=mesh,
        in_specs=(
            P("hid", "tok"),
            P("tok"),
            P("tok", "hid"),
            P("tok", "hid"),
            P("hid", "tok"),
            P(),
        ),
        out_specs=(P(("tok", "hid"), None), P(("tok", "hid"), None)),
        check_vma=False,
    )
```

profile of v0, /device:TPU:1, one launch (start us, length us, event | category | flops | bytes accessed | tf_op | source)
XLA Modules:
  0.0 691.0 jit_solution(11875496450596271961)
XLA Ops:
  7.2 0.0 copy-start
  7.2 0.0 reduce-scatter.3.cloned.1.call-start
  7.2 46.5 %all_gather.9 = bf16[512,512]{1,0:T(8,128)(2,1)S(1)} all-gather(bf16[16,512]{1,0:T(8,128)(2,1)} %param.6), channel_id=1, replica_groups=mesh['tok'=16,'hid'=32] {'hid'}, dimensions={0}, use_global_device_ids=true | all-gather | bytes 540672 | tf_op jit(solution)/shard_map/all_gather | solution.py:11
  53.7 0.2 copy.10
  53.9 0.2 multiply_reduce_fusion
  54.1 50.9 %psum.7 = f32[512]{0:T(512)S(1)} all-reduce(f32[512]{0:T(512)S(1)} %multiply_reduce_fusion), channel_id=1, replica_groups=mesh['tok'=16,'hid'=32] {'tok'}, use_global_device_ids=true, to_apply=%region_1.0 | all-reduce | flops 512 | bytes 4096 | tf_op jit(solution)/shard_map/psum | solution.py:14
  105.0 4.0 convolution_convert_fusion
  109.0 0.0 reduce-scatter.3.cloned.1.call-update
  109.0 0.0 copy-start.1
  109.0 0.0 reduce-scatter.5.cloned.1.call-start
  109.0 217.4 %reduce-scatter.3.cloned.1.call-done = bf16[32,1792]{1,0:T(8,128)(2,1)} async-done(((bf16[512,1792]{1,0:T(8,128)(2,1)}), bf16[32,1792]{1,0:T(8,128)(2,1)}) %reduce-scatter.3.cloned.1.call-update) | async-done | bytes 114704 | tf_op jit(solution)/shard_map/reduce_scatter | solution.py:19
  326.4 0.9 convert_element_type.33
  327.4 57.8 %all_gather.10 = bf16[512,896]{1,0:T(8,128)(2,1)S(1)} all-gather(bf16[32,896]{1,0:T(8,128)(2,1)S(1)} %fusion.7), channel_id=1, replica_groups=mesh['tok'=16,'hid'=32] {'tok'}, dimensions={0}, use_global_device_ids=true | all-gather | bytes 974848 | tf_op jit(solution)/shard_map/all_gather | solution.py:27
  385.2 1.6 convolution_convert_fusion.1
  386.7 0.0 reduce-scatter.5.cloned.1.call-update
  386.7 0.0 all-gather.2.cloned.1.call-start
  386.8 0.1 convert_element_type.30
  386.9 157.9 %reduce-scatter.5.cloned.1.call-done = bf16[512,16]{0,1:T(8,128)(2,1)} async-done(((bf16[512,512]{0,1:T(8,128)(2,1)}), bf16[512,16]{0,1:T(8,128)(2,1)}) %reduce-scatter.5.cloned.1.call-update) | async-done | bytes 16400 | tf_op jit(solution)/shard_map/reduce_scatter | solution.py:34
  544.9 1.3 add_convert_fusion
  546.2 0.0 all-gather.2.cloned.1.call-update
  546.2 0.1 convert_reduce_fusion
  546.3 1.5 convolution_divide_fusion
  547.8 130.1 %all-gather.2.cloned.1.call-done = bf16[512,8192]{0,1:T(8,128)(2,1)} async-done(((bf16[512,16]{0,1:T(8,128)(2,1)}), bf16[512,8192]{0,1:T(8,128)(2,1)}) %all-gather.2.cloned.1.call-update) | async-done | bytes 8388624 | tf_op jit(solution)/shard_map/all_gather | solution.py:41
  677.9 6.5 convolution_multiply_fusion
  (5 shorter events, 0.1 us)
Async XLA Ops:
  7.2 378.0 %copy-start = (bf16[896,512]{1,0:T(8,128)(2,1)S(1)}, bf16[896,512]{1,0:T(8,128)(2,1)}, u32[]{:S(2)}) copy-start(bf16[896,512]{1,0:T(8,128)(2,1)} %param.10) | copy-start | bytes 2752516
  7.2 319.2 %reduce-scatter.3.cloned.1.call-start = ((), (), s32[]{:S(2)}) async-start(), calls=%async_computation.2 | async-start | bytes 1949696 | tf_op jit(solution)/shard_map/reduce_scatter | solution.py:19
  109.0 437.2 %copy-start.1 = (s32[512]{0:T(512)S(1)}, s32[512]{0:T(512)}, u32[]{:S(2)}) copy-start(s32[512]{0:T(512)} %param.11) | copy-start | bytes 6148
  109.0 435.9 %reduce-scatter.5.cloned.1.call-start = ((), (), s32[]{:S(2)}) async-start(), calls=%async_computation.3 | async-start | bytes 540672 | tf_op jit(solution)/shard_map/reduce_scatter | solution.py:34
  386.7 291.2 %all-gather.2.cloned.1.call-start = ((), (), s32[]{:S(2)}) async-start(), calls=%async_computation.4 | async-start | bytes 8404992 | tf_op jit(solution)/shard_map/all_gather | solution.py:41
Sparse Core Ops, SparseCore 0:
  109.1 217.2 reduce-scatter.2
  386.9 157.9 reduce-scatter.4
  549.3 128.5 all-gather.1
where the time goes:
time: 691 us
  waiting for transfers between devices  505 us (73%)
  blocking collectives  155 us (22%)
  between operations  13.8 us (2%)
  matrix products  13.5 us (2%)
    reduce_scatter x1, waiting for transfers between devices, on_device(): lax.psum_scatter(jnp.dot(normed, both_weights, preferred_element_type=jnp...  217 us
    reduce_scatter x1, waiting for transfers between devices, on_device(): lax.psum_scatter(partial_out.astype(jnp.bfloat16), 'hid', scatter_dimensi...  158 us
    all_gather x1, waiting for transfers between devices, on_device(): lax.all_gather(resid_cols, ('tok', 'hid'), axis=1, tiled=True)  130 us
    all_gather x1, blocking collectives, on_device(): lax.all_gather(hidden, 'tok', axis=0, tiled=True)  57.8 us
    psum x1, blocking collectives, on_device(): total_sq = lax.psum(local_sq, 'tok')  50.9 us
    all_gather x1, blocking collectives, on_device(): gathered = lax.all_gather(resid_in, 'hid', axis=0, tiled=True)  46.5 us
  transfers between devices with their start and end apart: 3, of which 3 were waited for; matrix products, arithmetic and copies ran while one was open for 0% of the time, Pallas kernels for 0%

commit v1 on v0

--- a/solution.py
+++ b/solution.py
@@ -11,7 +11,8 @@
     gathered = lax.all_gather(resid_in, "hid", axis=0, tiled=True)
     xf = gathered.astype(jnp.float32)
     local_sq = jnp.sum(xf * xf, axis=1)
-    total_sq = lax.psum(local_sq, "tok")
+    parts = lax.all_gather(local_sq, "tok")
+    total_sq = jnp.sum(parts, axis=0)
     scale_rows = lax.rsqrt(total_sq / float(D) + 1e-05)
     normed = (xf * scale_rows[:, None] * norm_gain[None, :]).astype(jnp.bfloat16)
     both_weights = jnp.concatenate([gate_weight, up_weight], axis=1)

time: 691 us -> 689 us (level)
    psum x1 -> x0, blocking collectives: 50.9 us -> none  [on_device(): total_sq = lax.psum(local_sq, 'tok')]
    all_gather x0 -> x1, blocking collectives: none -> 49.9 us  [on_device(): parts = lax.all_gather(local_sq, 'tok')]
where the time goes in v1:
time: 689 us; the launch traced here: 688 us
  waiting for transfers between devices  506 us (73%)
  blocking collectives  152 us (22%)
  between operations  13.8 us (2%)
  matrix products  13.5 us (2%)
    reduce_scatter x1, waiting for transfers between devices, on_device(): lax.psum_scatter(jnp.dot(normed, both_weights, preferred_element_type=jnp...  217 us
    reduce_scatter x1, waiting for transfers between devices, on_device(): lax.psum_scatter(partial_out.astype(jnp.bfloat16), 'hid', scatter_dimensi...  159 us
    all_gather x1, waiting for transfers between devices, on_device(): lax.all_gather(resid_cols, ('tok', 'hid'), axis=1, tiled=True)  130 us
    all_gather x1, blocking collectives, on_device(): lax.all_gather(hidden, 'tok', axis=0, tiled=True)  55.4 us
    all_gather x1, blocking collectives, on_device(): parts = lax.all_gather(local_sq, 'tok')  49.9 us
    all_gather x1, blocking collectives, on_device(): gathered = lax.all_gather(resid_in, 'hid', axis=0, tiled=True)  46.5 us
  transfers between devices with their start and end apart: 3, of which 3 were waited for; matrix products, arithmetic and copies ran while one was open for 0% of the time, Pallas kernels for 0%

profile of v1, /device:TPU:1, one launch (start us, length us, event | category | flops | bytes accessed | tf_op | source)
XLA Modules:
  0.0 688.3 jit_solution(2523648044745776266)
XLA Ops:
  7.2 0.0 copy-start
  7.2 0.0 reduce-scatter.3.cloned.1.call-start
  7.2 46.5 %all_gather.15 = bf16[512,512]{1,0:T(8,128)(2,1)S(1)} all-gather(bf16[16,512]{1,0:T(8,128)(2,1)} %param.6), channel_id=1, replica_groups=mesh['tok'=16,'hid'=32] {'hid'}, dimensions={0}, use_global_device_ids=true | all-gather | bytes 540672 | tf_op jit(solution)/shard_map/all_gather | solution.py:11
  53.7 0.2 copy.10
  53.9 0.2 multiply_reduce_fusion
  54.1 49.9 %all-gather.1 = f32[16,1,512]{2,1,0:T(1,128)S(1)} all-gather(f32[1,1,512]{2,1,0:T(1,128)S(1)} %bitcast.6), channel_id=2, replica_groups=mesh['tok'=16,'hid'=32] {'tok'}, dimensions={0}, use_global_device_ids=true | all-gather | bytes 34816 | tf_op jit(solution)/shard_map/all_gather | solution.py:14
  104.0 4.0 convolution_convert_fusion
  108.0 0.0 reduce-scatter.3.cloned.1.call-update
  108.0 0.0 copy-start.1
  108.0 0.0 reduce-scatter.5.cloned.1.call-start
  108.1 217.3 %reduce-scatter.3.cloned.1.call-done = bf16[32,1792]{1,0:T(8,128)(2,1)} async-done(((bf16[512,1792]{1,0:T(8,128)(2,1)}), bf16[32,1792]{1,0:T(8,128)(2,1)}) %reduce-scatter.3.cloned.1.call-update) | async-done | bytes 114704 | tf_op jit(solution)/shard_map/reduce_scatter | solution.py:20
  325.4 0.9 convert_element_type.33
  326.3 55.4 %all_gather.18 = bf16[512,896]{1,0:T(8,128)(2,1)S(1)} all-gather(bf16[32,896]{1,0:T(8,128)(2,1)S(1)} %fusion.7), channel_id=1, replica_groups=mesh['tok'=16,'hid'=32] {'tok'}, dimensions={0}, use_global_device_ids=true | all-gather | bytes 974848 | tf_op jit(solution)/shard_map/all_gather | solution.py:28
  381.8 1.6 convolution_convert_fusion.1
  383.3 0.0 reduce-scatter.5.cloned.1.call-update
  383.3 0.0 all-gather.4.cloned.1.call-start
  383.4 0.1 convert_element_type.30
  383.5 158.7 %reduce-scatter.5.cloned.1.call-done = bf16[512,16]{0,1:T(8,128)(2,1)} async-done(((bf16[512,512]{0,1:T(8,128)(2,1)}), bf16[512,16]{0,1:T(8,128)(2,1)}) %reduce-scatter.5.cloned.1.call-update) | async-done | bytes 16400 | tf_op jit(solution)/shard_map/reduce_scatter | solution.py:35
  542.3 1.3 add_convert_fusion
  543.6 0.0 all-gather.4.cloned.1.call-update
  543.6 0.1 convert_reduce_fusion
  543.7 1.5 convolution_divide_fusion
  545.2 130.1 %all-gather.4.cloned.1.call-done = bf16[512,8192]{0,1:T(8,128)(2,1)} async-done(((bf16[512,16]{0,1:T(8,128)(2,1)}), bf16[512,8192]{0,1:T(8,128)(2,1)}) %all-gather.4.cloned.1.call-update) | async-done | bytes 8388624 | tf_op jit(solution)/shard_map/all_gather | solution.py:42
  675.3 6.5 convolution_multiply_fusion
  (6 shorter events, 0.1 us)
Async XLA Ops:
  7.2 374.6 %copy-start = (bf16[896,512]{1,0:T(8,128)(2,1)S(1)}, bf16[896,512]{1,0:T(8,128)(2,1)}, u32[]{:S(2)}) copy-start(bf16[896,512]{1,0:T(8,128)(2,1)} %param.10) | copy-start | bytes 2752516
  7.2 318.2 %reduce-scatter.3.cloned.1.call-start = ((), (), s32[]{:S(2)}) async-start(), calls=%async_computation.2 | async-start | bytes 1949696 | tf_op jit(solution)/shard_map/reduce_scatter | solution.py:20
  108.0 435.6 %copy-start.1 = (s32[512]{0:T(512)S(1)}, s32[512]{0:T(512)}, u32[]{:S(2)}) copy-start(s32[512]{0:T(512)} %param.11) | copy-start | bytes 6148
  108.0 434.2 %reduce-scatter.5.cloned.1.call-start = ((), (), s32[]{:S(2)}) async-start(), calls=%async_computation.3 | async-start | bytes 540672 | tf_op jit(solution)/shard_map/reduce_scatter | solution.py:35
  383.3 292.0 %all-gather.4.cloned.1.call-start = ((), (), s32[]{:S(2)}) async-start(), calls=%async_computation.4 | async-start | bytes 8404992 | tf_op jit(solution)/shard_map/all_gather | solution.py:42
Sparse Core Ops, SparseCore 0:
  108.2 217.1 reduce-scatter.2
  383.5 158.7 reduce-scatter.4
  546.7 128.5 all-gather.3

commit v2 on v0

--- a/solution.py
+++ b/solution.py
@@ -2,6 +2,7 @@
 import jax.numpy as jnp
 from jax import lax
 from jax.sharding import PartitionSpec as P
+from jax.lax import all_to_all, axis_size
 
 D = 8192
 CLASSES = 64
@@ -36,9 +37,16 @@
     ).astype(jnp.float32)
     x_cols = lax.dynamic_slice_in_dim(xf, offset, panel, 1)
     resid_cols = (x_cols + summed).astype(jnp.bfloat16)
+
+    def time_screen(field_in):
+        return jnp.concatenate(
+            all_to_all(jnp.stack(axis_size(("tok", "hid")) * [field_in]), ("tok", "hid"), 0, 0),
+            axis=1,
+        )
+
     prod = lax.dot_general(
         resid_cols,
-        lax.all_gather(resid_cols, ("tok", "hid"), axis=1, tiled=True),
+        time_screen(resid_cols),
         (((0,), (0,)), ((), ())),
         preferred_element_type=jnp.float32,
     )

time: 691 us -> 767 us (1.11)
  waiting for transfers between devices: 505 us -> 560 us
  starting transfers between devices: 0.12 us -> 19.3 us
    all_to_all x0 -> x1, waiting for transfers between devices: none -> 185 us  [time_screen(): all_to_all(jnp.stack(axis_size(('tok', 'hid')) * [field_in]), ('tok', 'hi...]
    all_gather x1 -> x0, waiting for transfers between devices: 130 us -> none  [on_device(): lax.all_gather(resid_cols, ('tok', 'hid'), axis=1, tiled=True)]
    all_to_all x0 -> x1, starting transfers between devices: none -> 19.2 us  [time_screen(): all_to_all(jnp.stack(axis_size(('tok', 'hid')) * [field_in]), ('tok', 'hi...]
where the time goes in v2:
time: 767 us
  waiting for transfers between devices  560 us (73%)
  blocking collectives  155 us (20%)
  starting transfers between devices  19.3 us (3%)
  between operations  14.1 us (2%)
  matrix products  12.7 us (2%)
    reduce_scatter x1, waiting for transfers between devices, on_device(): lax.psum_scatter(jnp.dot(normed, both_weights, preferred_element_type=jnp...  217 us
    all_to_all x1, waiting for transfers between devices, time_screen(): all_to_all(jnp.stack(axis_size(('tok', 'hid')) * [field_in]), ('tok', 'hi...  185 us
    reduce_scatter x1, waiting for transfers between devices, on_device(): lax.psum_scatter(partial_out.astype(jnp.bfloat16), 'hid', scatter_dimensi...  157 us
    all_gather x1, blocking collectives, on_device(): lax.all_gather(hidden, 'tok', axis=0, tiled=True)  57.1 us
    psum x1, blocking collectives, on_device(): total_sq = lax.psum(local_sq, 'tok')  50.9 us
    all_gather x1, blocking collectives, on_device(): gathered = lax.all_gather(resid_in, 'hid', axis=0, tiled=True)  46.5 us
    all_to_all x1, starting transfers between devices, time_screen(): all_to_all(jnp.stack(axis_size(('tok', 'hid')) * [field_in]), ('tok', 'hi...  19.2 us
  transfers between devices with their start and end apart: 3, of which 3 were waited for; matrix products, arithmetic and copies ran while one was open for 0% of the time, Pallas kernels for 0%

profile of v2, /device:TPU:1, one launch (start us, length us, event | category | flops | bytes accessed | tf_op | source)
XLA Modules:
  0.0 767.1 jit_solution(6145148521660917136)
XLA Ops:
  7.2 0.0 copy-start
  7.2 0.0 reduce-scatter.3.cloned.1.call-start
  7.2 46.5 %all_gather.6 = bf16[512,512]{1,0:T(8,128)(2,1)S(1)} all-gather(bf16[16,512]{1,0:T(8,128)(2,1)} %param.6), channel_id=1, replica_groups=mesh['tok'=16,'hid'=32] {'hid'}, dimensions={0}, use_global_device_ids=true | all-gather | bytes 540672 | tf_op jit(solution)/shard_map/all_gather | solution.py:12
  53.7 0.2 copy.12
  53.9 0.2 multiply_reduce_fusion
  54.1 50.9 %psum.7 = f32[512]{0:T(512)S(1)} all-reduce(f32[512]{0:T(512)S(1)} %multiply_reduce_fusion), channel_id=1, replica_groups=mesh['tok'=16,'hid'=32] {'tok'}, use_global_device_ids=true, to_apply=%region_1.0 | all-reduce | flops 512 | bytes 4096 | tf_op jit(solution)/shard_map/psum | solution.py:15
  105.0 4.0 convolution_convert_fusion
  109.0 0.0 reduce-scatter.3.cloned.1.call-update
  109.0 0.0 reduce-scatter.5.cloned.1.call-start
  109.0 217.5 %reduce-scatter.3.cloned.1.call-done = bf16[32,1792]{1,0:T(8,128)(2,1)} async-done(((bf16[512,1792]{1,0:T(8,128)(2,1)}), bf16[32,1792]{1,0:T(8,128)(2,1)}) %reduce-scatter.3.cloned.1.call-update) | async-done | bytes 114704 | tf_op jit(solution)/shard_map/reduce_scatter | solution.py:20
  326.5 0.9 convert_element_type.33
  327.5 57.1 %all_gather.7 = bf16[512,896]{1,0:T(8,128)(2,1)S(1)} all-gather(bf16[32,896]{1,0:T(8,128)(2,1)S(1)} %fusion.7), channel_id=1, replica_groups=mesh['tok'=16,'hid'=32] {'tok'}, dimensions={0}, use_global_device_ids=true | all-gather | bytes 974848 | tf_op jit(solution)/shard_map/all_gather | solution.py:28
  384.6 0.0 copy-done
  384.6 1.6 convolution_convert_fusion.1
  386.2 0.0 reduce-scatter.5.cloned.1.call-update
  386.2 0.1 convert_element_type.30
  386.4 157.0 %reduce-scatter.5.cloned.1.call-done = bf16[512,16]{0,1:T(8,128)(2,1)} async-done(((bf16[512,512]{0,1:T(8,128)(2,1)}), bf16[512,16]{0,1:T(8,128)(2,1)}) %reduce-scatter.5.cloned.1.call-update) | async-done | bytes 16400 | tf_op jit(solution)/shard_map/reduce_scatter | solution.py:35
  543.4 0.7 add_convert_fusion
  544.1 4.3 stack.2
  548.4 19.2 %all-to-all-start = ((bf16[512,512,16]{1,2,0:T(8,128)(2,1)}), bf16[512,512,16]{1,2,0:T(8,128)(2,1)}, u32[]{:S(2)}, u32[]{:S(2)}) async-start(bf16[512,512,16]{1,2,0:T(8,128)(2,1)} %stack.2), calls=%async_computation.2 | async-start | bytes 16777216 | tf_op jit(solution)/shard_map/all_to_all | solution.py:43
  567.7 0.1 convert_reduce_fusion
  567.8 0.7 convolution_divide_fusion
  568.5 185.2 %all-to-all-done = bf16[512,512,16]{1,2,0:T(8,128)(2,1)} async-done(((bf16[512,512,16]{1,2,0:T(8,128)(2,1)}), bf16[512,512,16]{1,2,0:T(8,128)(2,1)}, u32[]{:S(2)}, u32[]{:S(2)}) %all-to-all-start) | async-done | bytes 8388640 | tf_op jit(solution)/shard_map/all_to_all | solution.py:43
  753.8 6.5 convolution_multiply_fusion
  (5 shorter events, 0.1 us)
Async XLA Ops:
  7.2 377.5 %copy-start = (bf16[896,512]{1,0:T(8,128)(2,1)S(1)}, bf16[896,512]{1,0:T(8,128)(2,1)}, u32[]{:S(2)}) copy-start(bf16[896,512]{1,0:T(8,128)(2,1)} %param.10) | copy-start | bytes 2752516
  7.2 319.3 %reduce-scatter.3.cloned.1.call-start = ((), (), s32[]{:S(2)}) async-start(), calls=%async_computation.3 | async-start | bytes 1949696 | tf_op jit(solution)/shard_map/reduce_scatter | solution.py:20
  109.0 434.4 %reduce-scatter.5.cloned.1.call-start = ((), (), s32[]{:S(2)}) async-start(), calls=%async_computation.4 | async-start | bytes 540672 | tf_op jit(solution)/shard_map/reduce_scatter | solution.py:35
  548.4 19.3 %copy-start.1 = (s32[512]{0:T(512)S(1)}, s32[512]{0:T(512)}, u32[]{:S(2)}) copy-start(s32[512]{0:T(512)} %param.11) | copy-start | bytes 6148
  548.4 205.4 %all-to-all-start = ((bf16[512,512,16]{1,2,0:T(8,128)(2,1)}), bf16[512,512,16]{1,2,0:T(8,128)(2,1)}, u32[]{:S(2)}, u32[]{:S(2)}) async-start(bf16[512,512,16]{1,2,0:T(8,128)(2,1)} %stack.2), calls=%async_computation.2 | async-start | bytes 16777216 | tf_op jit(solution)/shard_map/all_to_all | solution.py:43
Sparse Core Ops, SparseCore 0:
  109.1 217.3 reduce-scatter.2
  386.3 157.0 reduce-scatter.4
